TPU v7x, 32 devices: a whole 2x2x4 slice. The times are simulated.
32 devices in a mesh: req: 8 (over z, y), seq: 4 (over x, core).
Axes of the slice: x: 2, y: 2, z: 4, core: 2. Of those that a mesh axis runs over, the one named last changes fastest.
Arguments:
- prompt_query: bfloat16 [8, 4096, 1024], P('req', 'seq'), may hold values from -6 to 6
- prompt_key: bfloat16 [8, 4096, 1024], P('req', 'seq'), may hold values from -6 to 6
- prompt_value: bfloat16 [8, 4096, 2048], P('req', 'seq'), may hold values from -6 to 6
- prompt_gate_logit: bfloat16 [8, 4096, 1024], P('req', 'seq'), may hold values from -12 to 12
- prompt_out_gate: bfloat16 [8, 4096, 2048], P('req', 'seq'), may hold values from -6 to 6
- prompt_len: int32 [8], P('req'), may hold values from 1024 to 4096, as said below
- suffix_query: bfloat16 [32, 256, 1024], P('req'), may hold values from -6 to 6
- suffix_key: bfloat16 [32, 256, 1024], P('req'), may hold values from -6 to 6
- suffix_value: bfloat16 [32, 256, 2048], P('req', None, 'seq'), may hold values from -6 to 6
- suffix_gate_logit: bfloat16 [32, 256, 1024], P('req'), may hold values from -12 to 12
- suffix_out_gate: bfloat16 [32, 256, 2048], P('req', None, 'seq'), may hold values from -6 to 6
- suffix_len: int32 [32], P('req'), may hold values from 64 to 256, as said below
- request_group: int32 [32], P('req'), may hold values from 0 to 7, as said below
- norm_gain: float32 [512], replicated, may hold values from 0.1 to 1.9
Outputs:
- prompt_out: bfloat16 [8, 4096, 2048], P('req', 'seq')
- suffix_out: bfloat16 [32, 256, 2048], P('req', None, 'seq')
Inputs may be any that keep to these rules, and one draw needn't show every extreme that they name: `prompt_len`: some group's prompt fills all 4096 positions. `suffix_len`: some request's suffix fills all 256 positions. `request_group`: every group has at least one request.
All inputs are finite; a program needn't handle non-finite values.
Results may differ from a plain program's by a relative error of at most 0.001.
Values sent between devices are 32-bit elements; how exact they have to be, the bound alone decides.
A program may use at most 192 MiB of HBM per device.

v0:
```python
import functools

import jax
import jax.numpy as jnp
from jax import lax
from jax.experimental import pallas as pl
from jax.experimental.pallas import tpu as pltpu
from jax.sharding import PartitionSpec as P

HEAD_COUNT = 4
KEY_CHANNELS = 256
DVH = 512
CHUNK = 256
HALF = 128
SCALE = KEY_CHANNELS ** (-0.5)
epsilon = 1e-05
f32 = jnp.float32
bf16 = jnp.bfloat16

NN = (((1,), (0,)), ((), ()))
NT = (((1,), (1,)), ((), ()))
TN = (((0,), (0,)), ((), ()))


def dot(a, b, dims):
    return lax.dot_general(a, b, dims, preferred_element_type=f32)


def split(x):
    hi = x.astype(bf16)
    return hi, (x - hi.astype(f32)).astype(bf16)


def dot3(a, b, dims):
    return dot(a[0], b[0], dims) + (dot(a[0], b[1], dims) + dot(a[1], b[0], dims))


def decay_rates(logits):
    x = logits.astype(f32)
    return (jnp.minimum(x, 0.0) - jnp.log(1.0 + jnp.exp(-jnp.abs(x)))) * (1.0 / 16.0)


def running_sum(tri, decay):
    hi = decay.astype(bf16)
    rest = decay - hi.astype(f32)
    mid = rest.astype(bf16)
    low = (rest - mid.astype(f32)).astype(bf16)
    return dot(tri, hi, NN) + (dot(tri, mid, NN) + dot(tri, low, NN))


def column(row):
    turned = jnp.broadcast_to(row, (128, KEY_CHANNELS)).T
    return jnp.concatenate([turned] * (DVH // 128), axis=1)


def alive_column(first, length, rows):
    return (first + lax.broadcasted_iota(jnp.int32, (rows, 1), 0) < length).astype(f32)


def state_kernel(heads, info, k_ref, g_ref, v_ref, s_ref, o_ref):
    j = pl.program_id(1)
    alive = alive_column(info[0] + j * CHUNK, info[1], CHUNK)
    r = lax.broadcasted_iota(jnp.int32, (CHUNK, CHUNK), 0)
    c = lax.broadcasted_iota(jnp.int32, (CHUNK, CHUNK), 1)
    tri = (r >= c).astype(f32).astype(bf16)
    running = running_sum(tri, decay_rates(g_ref[0]) * alive)
    closing = running[CHUNK - 1 :]
    fading = split(k_ref[0].astype(f32) * alive * jnp.exp(closing - running))
    v = v_ref[0]
    update = dot(fading[0], v, TN) + dot(fading[1], v, TN)

    @pl.when(j == 0)
    def _():
        s_ref[0] = update
        o_ref[0] = closing

    @pl.when(j > 0)
    def _():
        s_ref[0] = s_ref[0] * column(jnp.exp(closing)) + update
        o_ref[0] += closing


def chunk_core(q, k, v, decay):
    r = lax.broadcasted_iota(jnp.int32, (CHUNK, CHUNK), 0)
    c = lax.broadcasted_iota(jnp.int32, (CHUNK, CHUNK), 1)
    causal = r >= c
    near = causal & ((r >= HALF) == (c >= HALF))
    running = running_sum(near.astype(f32).astype(bf16), decay)
    half_0 = 0.5 * running[HALF - 1 : HALF]
    half_1 = 0.5 * running[CHUNK - 1 :]
    shift_0 = running[:HALF] - half_0
    shift_1 = running[HALF:] - half_1
    e0, e1 = jnp.exp(half_0), jnp.exp(half_1)
    q0, q1 = q[:HALF] * jnp.exp(shift_0), q[HALF:] * jnp.exp(shift_1)
    k0, k1 = k[:HALF] * jnp.exp(-shift_0), k[HALF:] * jnp.exp(-shift_1)
    reach_1 = q1 * e1
    fade_0 = k0 * e0
    far = dot3(split(reach_1), split(fade_0), NT)
    diag_0 = dot3(split(q0), split(k0), NT)
    diag_1 = dot3(split(q1), split(k1), NT)
    tri = causal[:HALF, :HALF]
    top = jnp.concatenate([jnp.where(tri, diag_0, 0.0), jnp.zeros((HALF, HALF), f32)], axis=1)
    bottom = jnp.concatenate([far, jnp.where(tri, diag_1, 0.0)], axis=1)
    scores = split(jnp.concatenate([top, bottom], axis=0))
    attended = dot(scores[0], v, NN) + dot(scores[1], v, NN)
    reach = jnp.concatenate([q0 * e0, reach_1 * (e0 * e0)], axis=0)
    fade = jnp.concatenate([fade_0 * (e1 * e1), k1 * e1], axis=0)
    return attended, reach, fade, 2.0 * (half_0 + half_1)


def gated(attended, z, gain, alive):
    mean_square = jnp.mean(attended * attended, axis=-1, keepdims=True)
    factor = lax.rsqrt(mean_square * (SCALE * SCALE) + epsilon) * (SCALE * alive)
    z = z.astype(f32)
    return (attended * factor * gain * (z * jax.nn.sigmoid(z))).astype(bf16)


def prompt_kernel(info, q_ref, k_ref, g_ref, v_ref, z_ref, e_ref, gain_ref, out_ref, state):
    j = pl.program_id(1)

    @pl.when(j == 0)
    def _():
        state[...] = e_ref[0]

    alive = alive_column(info[0] + j * CHUNK, info[1], CHUNK)
    v = v_ref[0]
    attended, reach, fade, closing = chunk_core(
        q_ref[0].astype(f32),
        k_ref[0].astype(f32) * alive,
        v,
        decay_rates(g_ref[0]) * alive,
    )
    current = state[...]
    attended += dot3(split(reach), split(current), NN)
    out_ref[0] = gated(attended, z_ref[0], gain_ref[...], alive)

    @pl.when(j < pl.num_programs(1) - 1)
    def _():
        fades = split(fade)
        state[...] = current * column(jnp.exp(closing)) + (dot(fades[0], v, TN) + dot(fades[1], v, TN))


def suffix_local_kernel(head, q_ref, k_ref, g_ref, v_ref, a_ref, r_ref):
    attended, reach, _, _ = chunk_core(
        q_ref[0].astype(f32), k_ref[0].astype(f32), v_ref[0], decay_rates(g_ref[0])
    )
    a_ref[0] = attended
    r_ref[0] = reach


def suffix_final_kernel(group, length, a_ref, r_ref, s_ref, z_ref, gain_ref, out_ref):
    attended = a_ref[0] + dot3(split(r_ref[0]), split(s_ref[0]), NN)
    alive = alive_column(0, length[pl.program_id(0)], CHUNK)
    out_ref[0] = gated(attended, z_ref[0], gain_ref[...], alive)


def cost(flops, data):
    return pl.CostEstimate(flops=int(flops), bytes_accessed=int(data), transcendentals=0)


PARAMS = dict(vmem_limit_bytes=40 << 20)


def local_states(heads, info, k, g, v):
    rows = k.shape[1]
    n = heads.shape[0]
    narrow = pl.BlockSpec((1, CHUNK, KEY_CHANNELS), lambda i, j, heads, info: (0, j, heads[i]))
    wide = pl.BlockSpec((1, CHUNK, DVH), lambda i, j, heads, info: (0, j, heads[i]))
    return pl.pallas_call(
        state_kernel,
        grid_spec=pltpu.PrefetchScalarGridSpec(
            num_scalar_prefetch=2,
            grid=(n, rows // CHUNK),
            in_specs=[narrow, narrow, wide],
            out_specs=[
                pl.BlockSpec((1, KEY_CHANNELS, DVH), lambda i, j, heads, info: (i, 0, 0)),
                pl.BlockSpec((1, 1, KEY_CHANNELS), lambda i, j, heads, info: (i, 0, 0)),
            ],
        ),
        out_shape=[
            jax.ShapeDtypeStruct((n, KEY_CHANNELS, DVH), f32),
            jax.ShapeDtypeStruct((n, 1, KEY_CHANNELS), f32),
        ],
        compiler_params=pltpu.CompilerParams(**PARAMS),
        cost_estimate=cost(4e9, 5e6),
        name="local_states",
    )(heads, info, k, g, v)


def prompt_attention(info, q, k, g, v, z, entering, gain):
    rows = q.shape[1]
    narrow = pl.BlockSpec((1, CHUNK, KEY_CHANNELS), lambda h, j, info: (0, j, h))
    wide = pl.BlockSpec((1, CHUNK, DVH), lambda h, j, info: (0, j, h))
    return pl.pallas_call(
        prompt_kernel,
        grid_spec=pltpu.PrefetchScalarGridSpec(
            num_scalar_prefetch=1,
            grid=(HEAD_COUNT, rows // CHUNK),
            in_specs=[
                narrow,
                narrow,
                narrow,
                wide,
                wide,
                pl.BlockSpec((1, KEY_CHANNELS, DVH), lambda h, j, info: (h, 0, 0)),
                pl.BlockSpec((1, DVH), lambda h, j, info: (0, 0)),
            ],
            out_specs=wide,
            scratch_shapes=[pltpu.VMEM((KEY_CHANNELS, DVH), f32)],
        ),
        out_shape=jax.ShapeDtypeStruct(v.shape, bf16),
        compiler_params=pltpu.CompilerParams(**PARAMS),
        cost_estimate=cost(3e10, 2e7),
        name="prompt_attention",
    )(info, q, k, g, v, z, entering, gain)


def suffix_local(head, q, k, g, v):
    count = q.shape[0]
    narrow = pl.BlockSpec((1, CHUNK, KEY_CHANNELS), lambda i, head: (i, 0, head[0]))
    wide = pl.BlockSpec((1, CHUNK, DVH), lambda i, head: (i, 0, 0))
    return pl.pallas_call(
        suffix_local_kernel,
        grid_spec=pltpu.PrefetchScalarGridSpec(
            num_scalar_prefetch=1,
            grid=(count,),
            in_specs=[narrow, narrow, narrow, wide],
            out_specs=[wide, pl.BlockSpec((1, CHUNK, KEY_CHANNELS), lambda i, head: (i, 0, 0))],
        ),
        out_shape=[
            jax.ShapeDtypeStruct((count, CHUNK, DVH), f32),
            jax.ShapeDtypeStruct((count, CHUNK, KEY_CHANNELS), f32),
        ],
        compiler_params=pltpu.CompilerParams(**PARAMS),
        cost_estimate=cost(6e9, 4e6),
        name="suffix_local",
    )(head, q, k, g, v)


def suffix_final(group, length, attended, reach, finals, z, gain):
    count = attended.shape[0]
    wide = pl.BlockSpec((1, CHUNK, DVH), lambda i, group, length: (i, 0, 0))
    return pl.pallas_call(
        suffix_final_kernel,
        grid_spec=pltpu.PrefetchScalarGridSpec(
            num_scalar_prefetch=2,
            grid=(count,),
            in_specs=[
                wide,
                pl.BlockSpec((1, CHUNK, KEY_CHANNELS), lambda i, group, length: (i, 0, 0)),
                pl.BlockSpec((1, KEY_CHANNELS, DVH), lambda i, group, length: (group[i], 0, 0)),
                wide,
                pl.BlockSpec((1, DVH), lambda i, group, length: (0, 0)),
            ],
            out_specs=wide,
        ),
        out_shape=jax.ShapeDtypeStruct(z.shape, bf16),
        compiler_params=pltpu.CompilerParams(**PARAMS),
        cost_estimate=cost(4e9, 8e6),
        name="suffix_final",
    )(group, length, attended, reach, finals, z, gain)


def fade_state(offset, state):
    return jnp.exp(jnp.swapaxes(offset, -1, -2)) * state


def pick(array, index):
    return lax.dynamic_index_in_dim(array, index, 0, keepdims=False)


def local(
    prompt_query,
    prompt_key,
    prompt_value,
    prompt_gate_logit,
    prompt_out_gate,
    prompt_len,
    suffix_query,
    suffix_key,
    suffix_value,
    suffix_gate_logit,
    suffix_out_gate,
    suffix_len,
    request_group,
    norm_gain,
):
    rank = lax.axis_index("seq")
    side, chip = lax.rem(rank, 2), lax.div(rank, 2)
    rows = prompt_query.shape[1]
    info = jnp.stack([rank * rows, prompt_len[0]]).astype(jnp.int32)
    gain = norm_gain[None]
    both = jnp.arange(2, dtype=jnp.int32) * 2
    across_core = [(0, 1), (1, 0), (2, 3), (3, 2)]
    across_chip = [(0, 2), (1, 3), (2, 0), (3, 1)]

    send_state, send_offset = local_states(
        both + 1 - side, info, prompt_key, prompt_gate_logit, prompt_value
    )
    near_state = lax.ppermute(send_state, "seq", across_core)
    near_offset = lax.ppermute(send_offset, "seq", across_core)
    own_state, own_offset = local_states(
        both + side, info, prompt_key, prompt_gate_logit, prompt_value
    )
    last_offset = jnp.where(side == 0, near_offset, own_offset)
    first_state = jnp.where(side == 0, own_state, near_state)
    last_state = jnp.where(side == 0, near_state, own_state)
    chip_state = fade_state(last_offset, first_state) + last_state
    chip_offset = own_offset + near_offset
    kept_state, kept_offset = pick(chip_state, chip), pick(chip_offset, chip)
    far_state = lax.ppermute(pick(chip_state, 1 - chip), "seq", across_chip)
    far_offset = lax.ppermute(pick(chip_offset, 1 - chip), "seq", across_chip)
    early_state = jnp.where(chip == 0, kept_state, far_state)
    late_state = jnp.where(chip == 0, far_state, kept_state)
    late_offset = jnp.where(chip == 0, far_offset, kept_offset)
    final = fade_state(late_offset, early_state) + late_state
    finals = lax.all_gather(final[None], "req", axis=0, tiled=True)

    suffix_attended, suffix_reach = suffix_local(
        rank.astype(jnp.int32)[None], suffix_query, suffix_key, suffix_gate_logit, suffix_value
    )

    rest = lax.ppermute(kept_state, "seq", [(0, 2), (1, 3)])
    side_heads = jnp.stack([rest, far_state])
    core_heads = lax.ppermute(side_heads, "seq", [(2, 3), (3, 2)])
    core_own = lax.ppermute(own_state, "seq", [(0, 1), (2, 3)])
    second_chip = chip == 1
    second_core = side == 1
    enter_mine = jnp.where(second_chip, side_heads, 0.0)
    enter_other = jnp.where(second_chip, core_heads, 0.0)
    first_other_offset = lax.ppermute(own_offset, "seq", [(0, 1), (2, 3)])
    enter_mine = jnp.where(second_core, fade_state(near_offset, enter_mine) + near_state, enter_mine)
    enter_other = jnp.where(
        second_core, fade_state(first_other_offset, enter_other) + core_own, enter_other
    )
    even = jnp.where(second_core, enter_other, enter_mine)
    odd = jnp.where(second_core, enter_mine, enter_other)
    entering = jnp.stack([even, odd], axis=1).reshape(HEAD_COUNT, KEY_CHANNELS, DVH)
    prompt_result = prompt_attention(
        info,
        prompt_query,
        prompt_key,
        prompt_gate_logit,
        prompt_value,
        prompt_out_gate,
        entering,
        gain,
    )
    suffix_result = suffix_final(
        request_group, suffix_len, suffix_attended, suffix_reach, finals, suffix_out_gate, gain
    )
    return (prompt_result, suffix_result)


def solution(mesh):
    placed = (
        P("req", "seq", None),
        P("req", "seq", None),
        P("req", "seq", None),
        P("req", "seq", None),
        P("req", "seq", None),
        P("req"),
        P("req", None, None),
        P("req", None, None),
        P("req", None, "seq"),
        P("req", None, None),
        P("req", None, "seq"),
        P("req"),
        P("req"),
        P(),
    )
    return jax.shard_map(
        local,
        mesh=mesh,
        in_specs=placed,
        out_specs=(P("req", "seq", None), P("req", None, "seq")),
        check_vma=False,
    )
```

profile of v0, /device:TPU:0, one launch (start us, length us, event | category | flops | bytes accessed | tf_op | source)
XLA Modules:
  0.0 143.1 jit_solution(3358727038557598481)
XLA Ops:
  7.2 0.0 all-gather.3.cloned.1.call-start
  7.9 0.1 pad_add_fusion.info
  8.0 2.2 %copy-done = bf16[1,1024,2048]{2,1,0:T(8,128)(2,1)S(1)} copy-done((bf16[1,1024,2048]{2,1,0:T(8,128)(2,1)S(1)}, bf16[1,1024,2048]{2,1,0:T(8,128)(2,1)}, u32[]{:S(2)}) %copy-start) | copy-done | bytes 4194328
  10.1 1.6 %copy-done.8 = bf16[1,1024,1024]{2,1,0:T(8,128)(2,1)S(1)} copy-done((bf16[1,1024,1024]{2,1,0:T(8,128)(2,1)S(1)}, bf16[1,1024,1024]{2,1,0:T(8,128)(2,1)}, u32[]{:S(2)}) %copy-start.8) | copy-done | bytes 2097176
  11.7 1.6 %copy-done.11 = bf16[1,1024,1024]{2,1,0:T(8,128)(2,1)S(1)} copy-done((bf16[1,1024,1024]{2,1,0:T(8,128)(2,1)S(1)}, bf16[1,1024,1024]{2,1,0:T(8,128)(2,1)}, u32[]{:S(2)}) %copy-start.11) | copy-done | bytes 2097176
  13.3 10.0 %local_states.3 = (f32[2,256,512]{2,1,0:T(8,128)S(1)}, f32[2,1,256]{2,1,0:T(1,128)S(1)}) custom-call(s32[2]{0:T(128)S(1)} %get-tuple-element.21.heads, s32[2]{0:T(128)S(1)} %pad_add_fusion.info, bf16[1,1024,1024]{2,1,0:T(8,128)(2,1)S(1)} %copy-done.8, bf16[1,1024,1024]{2,1,0:T(8,128)(2,1)S(1)} %copy-done.11, bf16[1,1024,2048]{2,1,0:T(8,128)(2,1)S(1)} %copy-done), custom_call_target="tpu_custom_call" | custom-call | flops 4000000000 | bytes 5000000 | tf_op jit(solution)/shard_map/local_states/pallas_call | solution.py:169
  23.3 0.5 collective-permute-start.2
  23.8 0.1 collective-permute-start.1
  23.9 10.0 %local_states.2 = (f32[2,256,512]{2,1,0:T(8,128)S(1)}, f32[2,1,256]{2,1,0:T(1,128)S(1)}) custom-call(s32[2]{0:T(128)S(1)} %get-tuple-element.22.heads, s32[2]{0:T(128)S(1)} %pad_add_fusion.info, bf16[1,1024,1024]{2,1,0:T(8,128)(2,1)S(1)} %copy-done.9, bf16[1,1024,1024]{2,1,0:T(8,128)(2,1)S(1)} %copy-done.11, bf16[1,1024,2048]{2,1,0:T(8,128)(2,1)S(1)} %copy-done.1), custom_call_target="tpu_custom_call" | custom-call | flops 4000000000 | bytes 5000000 | tf_op jit(solution)/shard_map/local_states/pallas_call | solution.py:169
  33.9 0.0 copy-start.24
  34.0 0.3 select_add_fusion
  34.2 0.0 copy-start.23
  34.2 1.0 copy-done.23
  35.3 3.0 %collective-permute-start.4 = (f32[256,512]{1,0:T(8,128)S(1)}, f32[256,512]{1,0:T(8,128)S(1)}, u32[]{:S(2)}, u32[]{:S(2)}) collective-permute-start(f32[256,512]{1,0:T(8,128)S(1)} %dynamic-slice_bitcast_fusion), channel_id=1, source_target_pairs={{0,2},{1,3},{2,0},{3,1},{4,6},{5,7},{6,4},{7,5},{8,10},{9,11},{10,... | collective-permute-start | bytes 1572872 | tf_op jit(solution)/shard_map/ppermute | solution.py:311
  38.3 0.1 collective-permute-start.7
  38.4 12.1 %collective-permute-done.7 = f32[1,256]{1,0:T(1,128)S(1)} collective-permute-done((f32[1,256]{1,0:T(1,128)S(1)}, f32[1,256]{1,0:T(1,128)S(1)}, u32[]{:S(2)}, u32[]{:S(2)}) %collective-permute-start.7) | collective-permute-done | bytes 1056 | tf_op jit(solution)/shard_map/ppermute | solution.py:312
  50.5 0.8 copy-done.22
  51.3 2.4 %select_add_fusion.1 = (f32[256,512]{1,0:T(8,128)}, f32[256,512]{1,0:T(8,128)}) fusion(f32[256,512]{1,0:T(8,128)} %copy-done.22, f32[256]{0:T(256)S(1)} %bitcast.41, pred[]{:T(512)S(6)} %eq.19, f32[2,256,512]{2,1,0:T(8,128)} %copy-done.23, s32[]{:T(128)S(6)} %select_n.87), kind=kLoop, calls=%fused_computation.7 | loop fusion | flops 524288 | bytes 2098181 | tf_op jit(solution)/shard_map/add | solution.py:316
  53.7 0.0 all-gather.3.cloned.1.call-update
  53.7 0.0 copy-start.5
  53.7 3.8 %collective-permute-start.3 = (f32[256,512]{1,0:T(8,128)}, f32[256,512]{1,0:T(8,128)S(1)}, u32[]{:S(2)}, u32[]{:S(2)}) collective-permute-start(f32[256,512]{1,0:T(8,128)} %get-tuple-element.15), channel_id=1, source_target_pairs={{0,2},{1,3},{4,6},{5,7},{8,10},{9,11},{12,14},{13,15},{16,18},{17,... | collective-permute-start | bytes 1572872 | tf_op jit(solution)/shard_map/ppermute | solution.py:323
  57.6 2.3 %collective-permute-start.6 = (f32[2,256,512]{2,1,0:T(8,128)S(1)}, f32[2,256,512]{2,1,0:T(8,128)}, u32[]{:S(2)}, u32[]{:S(2)}) collective-permute-start(f32[2,256,512]{2,1,0:T(8,128)S(1)} %get-tuple-element.10), channel_id=1, source_target_pairs={{0,1},{2,3},{4,5},{6,7},{8,9},{10,11},{12,13},{14,15},{16,17},{18,... | collective-permute-start | bytes 3145736 | tf_op jit(solution)/shard_map/ppermute | solution.py:326
  59.8 8.5 %collective-permute-done.3 = f32[256,512]{1,0:T(8,128)S(1)} collective-permute-done((f32[256,512]{1,0:T(8,128)}, f32[256,512]{1,0:T(8,128)S(1)}, u32[]{:S(2)}, u32[]{:S(2)}) %collective-permute-start.3) | collective-permute-done | bytes 524320 | tf_op jit(solution)/shard_map/ppermute | solution.py:323
  68.4 2.3 %pad_maximum_fusion.1 = f32[2,256,512]{2,1,0:T(8,128)} fusion(f32[1,256,512]{2,1,0:T(8,128)} %bitcast.34, f32[1,256,512]{2,1,0:T(8,128)S(1)} %bitcast.36), kind=kLoop, calls=%fused_computation.1 | loop fusion | flops 262144 | bytes 2097152 | tf_op jit(solution)/shard_map/stack | solution.py:324
  70.7 1.7 %collective-permute-start.5 = (f32[2,256,512]{2,1,0:T(8,128)}, f32[2,256,512]{2,1,0:T(8,128)}, u32[]{:S(2)}, u32[]{:S(2)}) collective-permute-start(f32[2,256,512]{2,1,0:T(8,128)} %pad_maximum_fusion.1), channel_id=1, source_target_pairs={{2,3},{3,2},{6,7},{7,6},{10,11},{11,10},{14,15},{15,14},{18,19},{1... | collective-permute-start | bytes 3145736 | tf_op jit(solution)/shard_map/ppermute | solution.py:325
  72.4 1.3 collective-permute-start
  73.8 0.0 copy-start.6
  73.8 1.6 %copy-done.6 = bf16[4,256,1024]{2,1,0:T(8,128)(2,1)S(1)} copy-done((bf16[4,256,1024]{2,1,0:T(8,128)(2,1)S(1)}, bf16[4,256,1024]{2,1,0:T(8,128)(2,1)}, u32[]{:S(2)}) %copy-start.6) | copy-done | bytes 2097176
  75.4 1.2 copy-done.13
  76.6 5.0 %suffix_local.1 = (f32[4,256,512]{2,1,0:T(8,128)S(1)}, f32[4,256,256]{2,1,0:T(8,128)S(1)}) custom-call(s32[1]{0:T(128)} %bitcast.9.head, bf16[4,256,1024]{2,1,0:T(8,128)(2,1)S(1)} %copy-done.4, bf16[4,256,1024]{2,1,0:T(8,128)(2,1)S(1)} %copy-done.5, bf16[4,256,1024]{2,1,0:T(8,128)(2,1)S(1)} %copy-done.6, bf16[4,256,512]{2,1,0:T(8,128)(2,1)S(1)} %copy-done.13), custom_call_target="tpu_custom_call" | custom-call | flops 6000000000 | bytes 4000000 | tf_op jit(solution)/shard_map/suffix_local/pallas_call | solution.py:222
  81.6 1.4 copy-done.18
  83.0 1.0 copy-done.20
  84.0 0.0 copy-start.12
  84.0 2.4 %select_bitcast_fusion.1 = (f32[2,1,256,512]{3,2,0,1:T(8,128)S(1)}, f32[2,1,256,512]{3,2,0,1:T(8,128)S(1)}) fusion(pred[]{:T(512)S(6)} %eq.16, f32[2,256,512]{2,1,0:T(8,128)} %collective-permute-done.6, f32[2,256,512]{2,1,0:T(8,128)} %collective-permute-done.5, pred[]{:T(512)S(6)} %eq.17, f32[2,256]{1,0:T(2,128)S(1)} %bitcast.39, ...), kind=kLoop, calls=%fused_computation.3 | loop fusion | flops 2883584 | bytes 6295554 | tf_op jit(solution)/shard_map/stack | solution.py:338
  86.4 0.0 copy-start.7
  86.4 0.0 copy-start.10
  86.4 0.2 pad_maximum_fusion
  86.7 0.0 copy-start.2
  86.7 0.0 copy-start.15
  86.7 0.2 copy.16
  86.9 1.2 copy-done.7
  88.0 0.6 copy-done.10
  88.7 1.7 %copy-done.2 = bf16[1,1024,2048]{2,1,0:T(8,128)(2,1)S(1)} copy-done((bf16[1,1024,2048]{2,1,0:T(8,128)(2,1)S(1)}, bf16[1,1024,2048]{2,1,0:T(8,128)(2,1)}, u32[]{:S(2)}) %copy-start.2) | copy-done | bytes 4194328
  90.3 31.6 %prompt_attention.1 = bf16[1,1024,2048]{2,1,0:T(8,128)(2,1)} custom-call(s32[2]{0:T(128)S(1)} %pad_add_fusion.info, bf16[1,1024,1024]{2,1,0:T(8,128)(2,1)S(1)} %copy-done.7, bf16[1,1024,1024]{2,1,0:T(8,128)(2,1)S(1)} %copy-done.10, bf16[1,1024,1024]{2,1,0:T(8,128)(2,1)S(1)} %copy-done.12, bf16[1,1024,2048]{2,1,0:T(8,128)(2,1)S(1)} %copy-done.2, ...), custom_call_target="tpu_custom_call" | custom-call | flops 30000001024 | bytes 20000000 | tf_op jit(solution)/shard_map/prompt_attention/pallas_call | solution.py:194
  122.0 6.8 %all-gather.3.cloned.1.call-done = f32[2048,512]{1,0:T(8,128)} async-done(((f32[256,512]{1,0:T(8,128)}), f32[2048,512]{1,0:T(8,128)}) %all-gather.3.cloned.1.call-update) | async-done | bytes 4194320 | tf_op jit(solution)/shard_map/all_gather | solution.py:317
  128.8 2.2 %copy-done.3 = f32[2048,512]{1,0:T(8,128)S(1)} copy-done((f32[2048,512]{1,0:T(8,128)S(1)}, f32[2048,512]{1,0:T(8,128)}, u32[]{:S(2)}) %copy-start.3) | copy-done | bytes 4194328
  131.0 1.6 %copy-done.19 = f32[4,256,512]{2,1,0:T(8,128)S(1)} copy-done((f32[4,256,512]{2,1,0:T(8,128)S(1)}, f32[4,256,512]{2,1,0:T(8,128)}, u32[]{:S(2)}) %copy-start.19) | copy-done | bytes 2097176
  132.6 3.7 %suffix_final.1 = bf16[4,256,512]{2,1,0:T(8,128)(2,1)} custom-call(s32[4]{0:T(128)S(1)} %copy-done.16, s32[4]{0:T(128)S(1)} %copy-done.17, f32[4,256,512]{2,1,0:T(8,128)S(1)} %copy-done.19, f32[4,256,256]{2,1,0:T(8,128)S(1)} %copy-done.21, f32[8,256,512]{2,1,0:T(8,128)S(1)} %bitcast.31, bf16[4,256,512]{2,1,0:T(8,128)(2,1)S(1)} %copy-done.14, ...), custom_call_target="tpu_custom_call" | custom-call | flops 4000000000 | bytes 8000000 | tf_op jit(solution)/shard_map/suffix_final/pallas_call | solution.py:243
  (44 shorter events, 0.1 us)
Async XLA Ops:
  7.2 121.6 %all-gather.3.cloned.1.call-start = ((), (), s32[]{:S(2)}) async-start(), calls=%async_computation | async-start | bytes 4718592 | tf_op jit(solution)/shard_map/all_gather | solution.py:317
  8.0 2.2 %copy-start = (bf16[1,1024,2048]{2,1,0:T(8,128)(2,1)S(1)}, bf16[1,1024,2048]{2,1,0:T(8,128)(2,1)}, u32[]{:S(2)}) copy-start(bf16[1,1024,2048]{2,1,0:T(8,128)(2,1)} %v_ref.6) | copy-start | bytes 12582916
  10.1 1.6 %copy-start.8 = (bf16[1,1024,1024]{2,1,0:T(8,128)(2,1)S(1)}, bf16[1,1024,1024]{2,1,0:T(8,128)(2,1)}, u32[]{:S(2)}) copy-start(bf16[1,1024,1024]{2,1,0:T(8,128)(2,1)} %k_ref.6) | copy-start | bytes 6291460
  11.7 1.6 %copy-start.11 = (bf16[1,1024,1024]{2,1,0:T(8,128)(2,1)S(1)}, bf16[1,1024,1024]{2,1,0:T(8,128)(2,1)}, u32[]{:S(2)}) copy-start(bf16[1,1024,1024]{2,1,0:T(8,128)(2,1)} %g_ref.6) | copy-start | bytes 6291460
  13.3 10.6 %copy-start.1 = (bf16[1,1024,2048]{2,1,0:T(8,128)(2,1)S(1)}, bf16[1,1024,2048]{2,1,0:T(8,128)(2,1)}, u32[]{:S(2)}) copy-start(bf16[1,1024,2048]{2,1,0:T(8,128)(2,1)} %v_ref.6) | copy-start | bytes 12582916
  13.3 10.6 %copy-start.9 = (bf16[1,1024,1024]{2,1,0:T(8,128)(2,1)S(1)}, bf16[1,1024,1024]{2,1,0:T(8,128)(2,1)}, u32[]{:S(2)}) copy-start(bf16[1,1024,1024]{2,1,0:T(8,128)(2,1)} %k_ref.6) | copy-start | bytes 6291460
  23.3 10.6 %collective-permute-start.2 = (f32[2,256,512]{2,1,0:T(8,128)S(1)}, f32[2,256,512]{2,1,0:T(8,128)S(1)}, u32[]{:S(2)}, u32[]{:S(2)}) collective-permute-start(f32[2,256,512]{2,1,0:T(8,128)S(1)} %get-tuple-element.11), channel_id=1, source_target_pairs={{0,1},{1,0},{2,3},{3,2},{4,5},{5,4},{6,7},{7,6},{8,9},{9,8},{10,11... | collective-permute-start | bytes 3145736 | tf_op jit(solution)/shard_map/ppermute | solution.py:300
  23.8 10.1 %collective-permute-start.1 = (f32[2,1,256]{2,1,0:T(1,128)S(1)}, f32[2,1,256]{2,1,0:T(1,128)S(1)}, u32[]{:S(2)}, u32[]{:S(2)}) collective-permute-start(f32[2,1,256]{2,1,0:T(1,128)S(1)} %get-tuple-element.9), channel_id=1, source_target_pairs={{0,1},{1,0},{2,3},{3,2},{4,5},{5,4},{6,7},{7,6},{8,9},{9,8},{10,11... | collective-permute-start | bytes 6152 | tf_op jit(solution)/shard_map/ppermute | solution.py:301
  33.9 1.4 copy-start.24
  34.2 1.0 copy-start.23
  35.3 15.2 %collective-permute-start.4 = (f32[256,512]{1,0:T(8,128)S(1)}, f32[256,512]{1,0:T(8,128)S(1)}, u32[]{:S(2)}, u32[]{:S(2)}) collective-permute-start(f32[256,512]{1,0:T(8,128)S(1)} %dynamic-slice_bitcast_fusion), channel_id=1, source_target_pairs={{0,2},{1,3},{2,0},{3,1},{4,6},{5,7},{6,4},{7,5},{8,10},{9,11},{10,... | collective-permute-start | bytes 1572872 | tf_op jit(solution)/shard_map/ppermute | solution.py:311
  38.3 12.2 %collective-permute-start.7 = (f32[1,256]{1,0:T(1,128)S(1)}, f32[1,256]{1,0:T(1,128)S(1)}, u32[]{:S(2)}, u32[]{:S(2)}) collective-permute-start(f32[1,256]{1,0:T(1,128)S(1)} %dynamic-slice_bitcast_fusion.2), channel_id=1, source_target_pairs={{0,2},{1,3},{2,0},{3,1},{4,6},{5,7},{6,4},{7,5},{8,10},{9,11},{10,... | collective-permute-start | bytes 3080 | tf_op jit(solution)/shard_map/ppermute | solution.py:312
  50.5 0.8 copy-start.22
  51.3 22.4 %copy-start.4 = (bf16[4,256,1024]{2,1,0:T(8,128)(2,1)S(1)}, bf16[4,256,1024]{2,1,0:T(8,128)(2,1)}, u32[]{:S(2)}) copy-start(bf16[4,256,1024]{2,1,0:T(8,128)(2,1)} %q_ref.3) | copy-start | bytes 6291460
  53.7 20.0 %copy-start.5 = (bf16[4,256,1024]{2,1,0:T(8,128)(2,1)S(1)}, bf16[4,256,1024]{2,1,0:T(8,128)(2,1)}, u32[]{:S(2)}) copy-start(bf16[4,256,1024]{2,1,0:T(8,128)(2,1)} %k_ref.7) | copy-start | bytes 6291460
  53.7 14.6 %collective-permute-start.3 = (f32[256,512]{1,0:T(8,128)}, f32[256,512]{1,0:T(8,128)S(1)}, u32[]{:S(2)}, u32[]{:S(2)}) collective-permute-start(f32[256,512]{1,0:T(8,128)} %get-tuple-element.15), channel_id=1, source_target_pairs={{0,2},{1,3},{4,6},{5,7},{8,10},{9,11},{12,14},{13,15},{16,18},{17,... | collective-permute-start | bytes 1572872 | tf_op jit(solution)/shard_map/ppermute | solution.py:323
  57.6 26.4 %collective-permute-start.6 = (f32[2,256,512]{2,1,0:T(8,128)S(1)}, f32[2,256,512]{2,1,0:T(8,128)}, u32[]{:S(2)}, u32[]{:S(2)}) collective-permute-start(f32[2,256,512]{2,1,0:T(8,128)S(1)} %get-tuple-element.10), channel_id=1, source_target_pairs={{0,1},{2,3},{4,5},{6,7},{8,9},{10,11},{12,13},{14,15},{16,17},{18,... | collective-permute-start | bytes 3145736 | tf_op jit(solution)/shard_map/ppermute | solution.py:326
  68.4 5.4 %copy-start.25 = (f32[256,512]{1,0:T(8,128)}, f32[256,512]{1,0:T(8,128)S(1)}, u32[]{:S(2)}) copy-start(f32[256,512]{1,0:T(8,128)S(1)} %collective-permute-done.3) | copy-start | bytes 1572868
  70.7 13.3 %collective-permute-start.5 = (f32[2,256,512]{2,1,0:T(8,128)}, f32[2,256,512]{2,1,0:T(8,128)}, u32[]{:S(2)}, u32[]{:S(2)}) collective-permute-start(f32[2,256,512]{2,1,0:T(8,128)} %pad_maximum_fusion.1), channel_id=1, source_target_pairs={{2,3},{3,2},{6,7},{7,6},{10,11},{11,10},{14,15},{15,14},{18,19},{1... | collective-permute-start | bytes 3145736 | tf_op jit(solution)/shard_map/ppermute | solution.py:325
  72.4 11.5 %collective-permute-start = (f32[2,1,256]{2,1,0:T(1,128)S(1)}, f32[2,1,256]{2,1,0:T(1,128)S(1)}, u32[]{:S(2)}, u32[]{:S(2)}) collective-permute-start(f32[2,1,256]{2,1,0:T(1,128)S(1)} %get-tuple-element.8), channel_id=1, source_target_pairs={{0,1},{2,3},{4,5},{6,7},{8,9},{10,11},{12,13},{14,15},{16,17},{18,... | collective-permute-start | bytes 6152 | tf_op jit(solution)/shard_map/ppermute | solution.py:331
  73.8 1.6 %copy-start.6 = (bf16[4,256,1024]{2,1,0:T(8,128)(2,1)S(1)}, bf16[4,256,1024]{2,1,0:T(8,128)(2,1)}, u32[]{:S(2)}) copy-start(bf16[4,256,1024]{2,1,0:T(8,128)(2,1)} %g_ref.7) | copy-start | bytes 6291460
  75.4 1.2 copy-start.13
  81.6 1.4 copy-start.18
  83.0 1.0 copy-start.20
  84.0 2.9 %copy-start.12 = (bf16[1,1024,1024]{2,1,0:T(8,128)(2,1)S(1)}, bf16[1,1024,1024]{2,1,0:T(8,128)(2,1)}, u32[]{:S(2)}) copy-start(bf16[1,1024,1024]{2,1,0:T(8,128)(2,1)} %g_ref.6) | copy-start | bytes 6291460
  86.4 1.6 %copy-start.7 = (bf16[1,1024,1024]{2,1,0:T(8,128)(2,1)S(1)}, bf16[1,1024,1024]{2,1,0:T(8,128)(2,1)}, u32[]{:S(2)}) copy-start(bf16[1,1024,1024]{2,1,0:T(8,128)(2,1)} %q_ref.2) | copy-start | bytes 6291460
  86.4 2.2 %copy-start.10 = (bf16[1,1024,1024]{2,1,0:T(8,128)(2,1)S(1)}, bf16[1,1024,1024]{2,1,0:T(8,128)(2,1)}, u32[]{:S(2)}) copy-start(bf16[1,1024,1024]{2,1,0:T(8,128)(2,1)} %k_ref.6) | copy-start | bytes 6291460
  86.7 3.7 %copy-start.2 = (bf16[1,1024,2048]{2,1,0:T(8,128)(2,1)S(1)}, bf16[1,1024,2048]{2,1,0:T(8,128)(2,1)}, u32[]{:S(2)}) copy-start(bf16[1,1024,2048]{2,1,0:T(8,128)(2,1)} %v_ref.6) | copy-start | bytes 12582916
  86.7 3.6 %copy-start.15 = (f32[512]{0:T(512)S(1)}, f32[512]{0:T(512)}, u32[]{:S(2)}) copy-start(f32[512]{0:T(512)} %param.27) | copy-start | bytes 6148
  90.3 38.5 %copy-start.14 = (bf16[4,256,512]{2,1,0:T(8,128)(2,1)S(1)}, bf16[4,256,512]{2,1,0:T(8,128)(2,1)}, u32[]{:S(2)}) copy-start(bf16[4,256,512]{2,1,0:T(8,128)(2,1)} %z_ref.3) | copy-start | bytes 3145732
  90.3 38.5 %copy-start.16 = (s32[4]{0:T(128)S(1)}, s32[4]{0:T(128)}, u32[]{:S(2)}) copy-start(s32[4]{0:T(128)} %group.1) | copy-start | bytes 52
  90.3 38.5 %copy-start.17 = (s32[4]{0:T(128)S(1)}, s32[4]{0:T(128)}, u32[]{:S(2)}) copy-start(s32[4]{0:T(128)} %length.1) | copy-start | bytes 52
  90.3 38.5 %copy-start.21 = (f32[4,256,256]{2,1,0:T(8,128)S(1)}, f32[4,256,256]{2,1,0:T(8,128)}, u32[]{:S(2)}) copy-start(f32[4,256,256]{2,1,0:T(8,128)} %copy-done.20) | copy-start | bytes 3145732
  128.8 2.2 %copy-start.3 = (f32[2048,512]{1,0:T(8,128)S(1)}, f32[2048,512]{1,0:T(8,128)}, u32[]{:S(2)}) copy-start(f32[2048,512]{1,0:T(8,128)} %all-gather.3.cloned.1.call-done) | copy-start | bytes 12582916
  131.0 1.6 %copy-start.19 = (f32[4,256,512]{2,1,0:T(8,128)S(1)}, f32[4,256,512]{2,1,0:T(8,128)}, u32[]{:S(2)}) copy-start(f32[4,256,512]{2,1,0:T(8,128)} %copy-done.18) | copy-start | bytes 6291460
Sparse Core Ops, SparseCore 0:
  53.9 74.8 all-gather.2
where the time goes:
time: 144 us; the launch traced here: 143 us
  Pallas kernels  60.2 us (42%)
  waiting for transfers between devices  27.5 us (19%)
  local copies, waits for them, and re-layouts  19.9 us (14%)
  between operations  15 us (10%)
  starting transfers between devices  12.8 us (9%)
  other arithmetic  7.7 us (5%)
    pallas_call x1, Pallas kernels, prompt_attention(): pl.pallas_call(prompt_kernel, grid_spec=pltpu.PrefetchScalarGridSpec(num_...  31.6 us
    pallas_call x2, Pallas kernels, local_states(): pl.pallas_call(state_kernel, grid_spec=pltpu.PrefetchScalarGridSpec(num_s...  19.9 us
    unnamed x55, local copies, waits for them, and re-layouts  19.7 us
    ppermute x1, waiting for transfers between devices, local(): far_offset = lax.ppermute(pick(chip_offset, 1 - chip), 'seq', across_chip)  12.1 us
    ppermute x1, waiting for transfers between devices, local(): rest = lax.ppermute(kept_state, 'seq', [(0, 2), (1, 3)])  8.53 us
    all_gather x1, waiting for transfers between devices, local(): finals = lax.all_gather(final[None], 'req', axis=0, tiled=True)  6.82 us
    pallas_call x1, Pallas kernels, suffix_local(): pl.pallas_call(suffix_local_kernel, grid_spec=pltpu.PrefetchScalarGridSpe...  5.01 us
    ppermute x1, starting transfers between devices, local(): rest = lax.ppermute(kept_state, 'seq', [(0, 2), (1, 3)])  3.81 us
  transfers between devices with their start and end apart: 9, of which 3 were waited for; matrix products, arithmetic and copies ran while one was open for 4% of the time, Pallas kernels for 33%

commit v1 on v0

--- a/solution.py
+++ b/solution.py
@@ -41,11 +41,8 @@
 
 
 def running_sum(tri, decay):
-    hi = decay.astype(bf16)
-    rest = decay - hi.astype(f32)
-    mid = rest.astype(bf16)
-    low = (rest - mid.astype(f32)).astype(bf16)
-    return dot(tri, hi, NN) + (dot(tri, mid, NN) + dot(tri, low, NN))
+    hi, lo = split(decay)
+    return dot(tri, hi, NN) + dot(tri, lo, NN)
 
 
 def column(row):
@@ -58,26 +55,24 @@
 
 
 def state_kernel(heads, info, k_ref, g_ref, v_ref, s_ref, o_ref):
-    j = pl.program_id(1)
-    alive = alive_column(info[0] + j * CHUNK, info[1], CHUNK)
+    rows = k_ref.shape[1]
     r = lax.broadcasted_iota(jnp.int32, (CHUNK, CHUNK), 0)
     c = lax.broadcasted_iota(jnp.int32, (CHUNK, CHUNK), 1)
-    tri = (r >= c).astype(f32).astype(bf16)
-    running = running_sum(tri, decay_rates(g_ref[0]) * alive)
-    closing = running[CHUNK - 1 :]
-    fading = split(k_ref[0].astype(f32) * alive * jnp.exp(closing - running))
+    later = (r < c).astype(f32).astype(bf16)
+    after = jnp.zeros((1, KEY_CHANNELS), f32)
+    highs, lows = [], []
+    for j in reversed(range(rows // CHUNK)):
+        span = pl.ds(j * CHUNK, CHUNK)
+        alive = alive_column(info[0] + j * CHUNK, info[1], CHUNK)
+        decay = decay_rates(g_ref[0, span]) * alive
+        to_end = running_sum(later, decay)
+        high, low = split(k_ref[0, span].astype(f32) * alive * jnp.exp(to_end + after))
+        highs.insert(0, high)
+        lows.insert(0, low)
+        after += to_end[:1] + decay[:1]
     v = v_ref[0]
-    update = dot(fading[0], v, TN) + dot(fading[1], v, TN)
-
-    @pl.when(j == 0)
-    def _():
-        s_ref[0] = update
-        o_ref[0] = closing
-
-    @pl.when(j > 0)
-    def _():
-        s_ref[0] = s_ref[0] * column(jnp.exp(closing)) + update
-        o_ref[0] += closing
+    s_ref[0] = dot(jnp.concatenate(highs, axis=0), v, TN) + dot(jnp.concatenate(lows, axis=0), v, TN)
+    o_ref[0] = after
 
 
 def chunk_core(q, k, v, decay):
@@ -158,23 +153,23 @@
     return pl.CostEstimate(flops=int(flops), bytes_accessed=int(data), transcendentals=0)
 
 
-PARAMS = dict(vmem_limit_bytes=40 << 20)
+PARAMS = dict(vmem_limit_bytes=60 << 20)
 
 
 def local_states(heads, info, k, g, v):
     rows = k.shape[1]
     n = heads.shape[0]
-    narrow = pl.BlockSpec((1, CHUNK, KEY_CHANNELS), lambda i, j, heads, info: (0, j, heads[i]))
-    wide = pl.BlockSpec((1, CHUNK, DVH), lambda i, j, heads, info: (0, j, heads[i]))
+    narrow = pl.BlockSpec((1, rows, KEY_CHANNELS), lambda i, heads, info: (0, 0, heads[i]))
+    wide = pl.BlockSpec((1, rows, DVH), lambda i, heads, info: (0, 0, heads[i]))
     return pl.pallas_call(
         state_kernel,
         grid_spec=pltpu.PrefetchScalarGridSpec(
             num_scalar_prefetch=2,
-            grid=(n, rows // CHUNK),
+            grid=(n,),
             in_specs=[narrow, narrow, wide],
             out_specs=[
-                pl.BlockSpec((1, KEY_CHANNELS, DVH), lambda i, j, heads, info: (i, 0, 0)),
-                pl.BlockSpec((1, 1, KEY_CHANNELS), lambda i, j, heads, info: (i, 0, 0)),
+                pl.BlockSpec((1, KEY_CHANNELS, DVH), lambda i, heads, info: (i, 0, 0)),
+                pl.BlockSpec((1, 1, KEY_CHANNELS), lambda i, heads, info: (i, 0, 0)),
             ],
         ),
         out_shape=[

time: 144 us -> 130 us (0.903)
  local copies, waits for them, and re-layouts: 19.9 us -> 1.59 us
  waiting for transfers between devices: 27.5 us -> 37.5 us
  Pallas kernels: 60.2 us -> 56.5 us
  other arithmetic: 7.7 us -> 6.22 us
    unnamed x55 -> x5, local copies, waits for them, and re-layouts: 19.7 us -> 0.01 us
    all_gather x1, waiting for transfers between devices: 6.82 us -> 17.1 us  [local(): finals = lax.all_gather(final[None], 'req', axis=0, tiled=True)]
    pallas_call x2, Pallas kernels: 19.9 us -> 13 us  [local_states(): pl.pallas_call(state_kernel, grid_spec=pltpu.PrefetchScalarGridSpec(num_s...]
    pallas_call x1, Pallas kernels: 3.67 us -> 6.03 us  [suffix_final(): pl.pallas_call(suffix_final_kernel, grid_spec=pltpu.PrefetchScalarGridSpe...]
    another operation x1, other arithmetic: 2.34 us -> 0.07 us  [local(): side_heads = jnp.stack([rest, far_state])]
    pallas_call x1, Pallas kernels: 5.01 us -> 6.48 us  [suffix_local(): pl.pallas_call(suffix_local_kernel, grid_spec=pltpu.PrefetchScalarGridSpe...]
  transfers between devices with their start and end apart: 9 -> 9, of which waited for: 3 -> 3; matrix products, arithmetic and copies ran while one was open for 4% -> 3% of each run, Pallas kernels for 33% -> 34%
where the time goes in v1:
time: 130 us; the launch traced here: 129 us
  Pallas kernels  56.5 us (43%)
  waiting for transfers between devices  37.5 us (29%)
  between operations  14.8 us (11%)
  starting transfers between devices  12.6 us (10%)
  other arithmetic  6.22 us (5%)
  local copies, waits for them, and re-layouts  1.59 us (1%)
    pallas_call x1, Pallas kernels, prompt_attention(): pl.pallas_call(prompt_kernel, grid_spec=pltpu.PrefetchScalarGridSpec(num_...  31 us
    all_gather x1, waiting for transfers between devices, local(): finals = lax.all_gather(final[None], 'req', axis=0, tiled=True)  17.1 us
    pallas_call x2, Pallas kernels, local_states(): pl.pallas_call(state_kernel, grid_spec=pltpu.PrefetchScalarGridSpec(num_s...  13 us
    ppermute x1, waiting for transfers between devices, local(): far_offset = lax.ppermute(pick(chip_offset, 1 - chip), 'seq', across_chip)  12.1 us
    ppermute x1, waiting for transfers between devices, local(): rest = lax.ppermute(kept_state, 'seq', [(0, 2), (1, 3)])  8.2 us
    pallas_call x1, Pallas kernels, suffix_local(): pl.pallas_call(suffix_local_kernel, grid_spec=pltpu.PrefetchScalarGridSpe...  6.48 us
    pallas_call x1, Pallas kernels, suffix_final(): pl.pallas_call(suffix_final_kernel, grid_spec=pltpu.PrefetchScalarGridSpe...  6.03 us
    ppermute x1, starting transfers between devices, local(): rest = lax.ppermute(kept_state, 'seq', [(0, 2), (1, 3)])  3.68 us
  transfers between devices with their start and end apart: 9, of which 3 were waited for; matrix products, arithmetic and copies ran while one was open for 3% of the time, Pallas kernels for 34%

profile of v1, /device:TPU:0, one launch (start us, length us, event | category | flops | bytes accessed | tf_op | source)
XLA Modules:
  0.0 129.1 jit_solution(6462033140086741303)
XLA Ops:
  7.2 0.0 all-gather.3.cloned.1.call-start
  7.9 0.6 add_subtract_fusion
  8.4 0.7 pad_add_fusion.info
  9.1 6.5 %local_states.3 = (f32[2,256,512]{2,1,0:T(8,128)}, f32[2,1,256]{2,1,0:T(1,128)}) custom-call(s32[2]{0:T(128)} %get-tuple-element.21.heads, s32[2]{0:T(128)} %pad_add_fusion.info, bf16[1,1024,1024]{2,1,0:T(8,128)(2,1)} %k_ref.6, bf16[1,1024,1024]{2,1,0:T(8,128)(2,1)} %g_ref.6, bf16[1,1024,2048]{2,1,0:T(8,128)(2,1)} %v_ref.6), custom_call_target="tpu_custom_call" | custom-call | flops 4000000000 | bytes 5000000 | tf_op jit(solution)/shard_map/local_states/pallas_call | solution.py:164
  15.6 0.5 collective-permute-start.2
  16.0 0.1 collective-permute-start.1
  16.1 6.5 %local_states.2 = (f32[2,256,512]{2,1,0:T(8,128)}, f32[2,1,256]{2,1,0:T(1,128)}) custom-call(s32[2]{0:T(128)} %get-tuple-element.22.heads, s32[2]{0:T(128)} %pad_add_fusion.info, bf16[1,1024,1024]{2,1,0:T(8,128)(2,1)} %k_ref.6, bf16[1,1024,1024]{2,1,0:T(8,128)(2,1)} %g_ref.6, bf16[1,1024,2048]{2,1,0:T(8,128)(2,1)} %v_ref.6), custom_call_target="tpu_custom_call" | custom-call | flops 4000000000 | bytes 5000000 | tf_op jit(solution)/shard_map/local_states/pallas_call | solution.py:164
  22.6 0.0 collective-permute-done.1
  22.6 0.7 fusion.3
  23.3 0.0 collective-permute-done.2
  23.3 1.4 %select_add_fusion = f32[2,256,512]{2,1,0:T(8,128)S(1)} fusion(f32[2,256,512]{2,1,0:T(8,128)S(1)} %collective-permute-done.2, f32[2,256,512]{2,1,0:T(8,128)} %get-tuple-element.10, f32[2,256]{1,0:T(2,128)S(1)} %bitcast.37, pred[]{:T(512)S(6)} %eq.18), kind=kLoop, calls=%fused_computation.6 | loop fusion | flops 1048576 | bytes 3147777 | tf_op jit(solution)/shard_map/add | solution.py:303
  24.8 3.0 %collective-permute-start.4 = (f32[256,512]{1,0:T(8,128)S(1)}, f32[256,512]{1,0:T(8,128)S(1)}, u32[]{:S(2)}, u32[]{:S(2)}) collective-permute-start(f32[256,512]{1,0:T(8,128)S(1)} %dynamic-slice_bitcast_fusion), channel_id=1, source_target_pairs={{0,2},{1,3},{2,0},{3,1},{4,6},{5,7},{6,4},{7,5},{8,10},{9,11},{10,... | collective-permute-start | bytes 1572872 | tf_op jit(solution)/shard_map/ppermute | solution.py:306
  27.8 0.1 collective-permute-start.7
  27.9 12.1 %collective-permute-done.7 = f32[1,256]{1,0:T(1,128)S(1)} collective-permute-done((f32[1,256]{1,0:T(1,128)S(1)}, f32[1,256]{1,0:T(1,128)S(1)}, u32[]{:S(2)}, u32[]{:S(2)}) %collective-permute-start.7) | collective-permute-done | bytes 1056 | tf_op jit(solution)/shard_map/ppermute | solution.py:307
  40.0 0.0 collective-permute-done.4
  40.0 0.0 copy-start
  40.0 1.0 select_add_fusion.1
  41.0 0.0 all-gather.3.cloned.1.call-update
  41.0 3.7 %collective-permute-start.3 = (f32[256,512]{1,0:T(8,128)S(1)}, f32[256,512]{1,0:T(8,128)S(1)}, u32[]{:S(2)}, u32[]{:S(2)}) collective-permute-start(f32[256,512]{1,0:T(8,128)S(1)} %get-tuple-element.15), channel_id=1, source_target_pairs={{0,2},{1,3},{4,6},{5,7},{8,10},{9,11},{12,14},{13,15},{16,18},{17,... | collective-permute-start | bytes 1572872 | tf_op jit(solution)/shard_map/ppermute | solution.py:318
  44.7 2.3 %collective-permute-start.6 = (f32[2,256,512]{2,1,0:T(8,128)}, f32[2,256,512]{2,1,0:T(8,128)}, u32[]{:S(2)}, u32[]{:S(2)}) collective-permute-start(f32[2,256,512]{2,1,0:T(8,128)} %get-tuple-element.10), channel_id=1, source_target_pairs={{0,1},{2,3},{4,5},{6,7},{8,9},{10,11},{12,13},{14,15},{16,17},{18,... | collective-permute-start | bytes 3145736 | tf_op jit(solution)/shard_map/ppermute | solution.py:321
  47.0 8.2 %collective-permute-done.3 = f32[256,512]{1,0:T(8,128)S(1)} collective-permute-done((f32[256,512]{1,0:T(8,128)S(1)}, f32[256,512]{1,0:T(8,128)S(1)}, u32[]{:S(2)}, u32[]{:S(2)}) %collective-permute-start.3) | collective-permute-done | bytes 524320 | tf_op jit(solution)/shard_map/ppermute | solution.py:318
  55.2 0.1 pad_maximum_fusion.1
  55.3 1.7 %collective-permute-start.5 = (f32[2,256,512]{2,1,0:T(8,128)S(1)}, f32[2,256,512]{2,1,0:T(8,128)}, u32[]{:S(2)}, u32[]{:S(2)}) collective-permute-start(f32[2,256,512]{2,1,0:T(8,128)S(1)} %pad_maximum_fusion.1), channel_id=1, source_target_pairs={{2,3},{3,2},{6,7},{7,6},{10,11},{11,10},{14,15},{15,14},{18,19},{1... | collective-permute-start | bytes 3145736 | tf_op jit(solution)/shard_map/ppermute | solution.py:320
  57.0 0.0 copy-done
  57.0 1.3 collective-permute-start
  58.3 6.5 %suffix_local.1 = (f32[4,256,512]{2,1,0:T(8,128)}, f32[4,256,256]{2,1,0:T(8,128)}) custom-call(s32[1]{0:T(128)} %bitcast.9.head, bf16[4,256,1024]{2,1,0:T(8,128)(2,1)} %q_ref.3, bf16[4,256,1024]{2,1,0:T(8,128)(2,1)} %k_ref.7, bf16[4,256,1024]{2,1,0:T(8,128)(2,1)} %g_ref.7, bf16[4,256,512]{2,1,0:T(8,128)(2,1)} %v_ref.7), custom_call_target="tpu_custom_call" | custom-call | flops 6000000000 | bytes 4000000 | tf_op jit(solution)/shard_map/suffix_local/pallas_call | solution.py:217
  64.8 0.0 collective-permute-done
  64.8 0.0 collective-permute-done.6
  64.8 0.0 collective-permute-done.5
  64.8 1.6 %select_bitcast_fusion.1 = (f32[2,1,256,512]{3,2,0,1:T(8,128)S(1)}, f32[2,1,256,512]{3,2,0,1:T(8,128)S(1)}) fusion(pred[]{:T(512)S(6)} %eq.16, f32[2,256,512]{2,1,0:T(8,128)} %collective-permute-done.6, f32[2,256,512]{2,1,0:T(8,128)} %collective-permute-done.5, pred[]{:T(512)S(6)} %eq.17, f32[2,256]{1,0:T(2,128)S(1)} %bitcast.36, ...), kind=kLoop, calls=%fused_computation.3 | loop fusion | flops 2883584 | bytes 6295554 | tf_op jit(solution)/shard_map/stack | solution.py:333
  66.4 0.2 pad_maximum_fusion
  66.6 1.5 %copy.16 = f32[2,2,256,512]{3,2,1,0:T(8,128)} copy(f32[2,2,256,512]{3,2,0,1:T(8,128)S(1)} %pad_maximum_fusion) | data formatting | bytes 4194304 | tf_op jit(solution)/shard_map/stack | solution.py:333
  68.2 31.0 %prompt_attention.1 = bf16[1,1024,2048]{2,1,0:T(8,128)(2,1)} custom-call(s32[2]{0:T(128)} %pad_add_fusion.info, bf16[1,1024,1024]{2,1,0:T(8,128)(2,1)} %q_ref.2, bf16[1,1024,1024]{2,1,0:T(8,128)(2,1)} %k_ref.6, bf16[1,1024,1024]{2,1,0:T(8,128)(2,1)} %g_ref.6, bf16[1,1024,2048]{2,1,0:T(8,128)(2,1)} %v_ref.6, bf16[1,1024,2048]{2,1,0:T(8,128)(2,1)} %z_ref.2, ...), custom_call_target="tpu_custom_call" | custom-call | flops 30000001024 | bytes 20000000 | tf_op jit(solution)/shard_map/prompt_attention/pallas_call | solution.py:189
  99.1 17.1 %all-gather.3.cloned.1.call-done = f32[2048,512]{1,0:T(8,128)} async-done(((f32[256,512]{1,0:T(8,128)}), f32[2048,512]{1,0:T(8,128)}) %all-gather.3.cloned.1.call-update) | async-done | bytes 4194320 | tf_op jit(solution)/shard_map/all_gather | solution.py:312
  116.3 6.0 %suffix_final.1 = bf16[4,256,512]{2,1,0:T(8,128)(2,1)} custom-call(s32[4]{0:T(128)} %group.1, s32[4]{0:T(128)} %length.1, f32[4,256,512]{2,1,0:T(8,128)} %get-tuple-element.12.a_ref, f32[4,256,256]{2,1,0:T(8,128)} %get-tuple-element.13.r_ref, f32[8,256,512]{2,1,0:T(8,128)} %bitcast.39, bf16[4,256,512]{2,1,0:T(8,128)(2,1)} %z_ref.3, f32[1,512]{1,0:T(1,128)} %bitcast.41), custom_call_target="tpu_custom_call" | custom-call | flops 4000000000 | bytes 8000000 | tf_op jit(solution)/shard_map/suffix_final/pallas_call | solution.py:238
  (7 shorter events, 0.1 us)
Async XLA Ops:
  7.2 109.1 %all-gather.3.cloned.1.call-start = ((), (), s32[]{:S(2)}) async-start(), calls=%async_computation | async-start | bytes 4718592 | tf_op jit(solution)/shard_map/all_gather | solution.py:312
  15.6 7.7 %collective-permute-start.2 = (f32[2,256,512]{2,1,0:T(8,128)}, f32[2,256,512]{2,1,0:T(8,128)S(1)}, u32[]{:S(2)}, u32[]{:S(2)}) collective-permute-start(f32[2,256,512]{2,1,0:T(8,128)} %get-tuple-element.11), channel_id=1, source_target_pairs={{0,1},{1,0},{2,3},{3,2},{4,5},{5,4},{6,7},{7,6},{8,9},{9,8},{10,11... | collective-permute-start | bytes 3145736 | tf_op jit(solution)/shard_map/ppermute | solution.py:295
  16.0 6.6 %collective-permute-start.1 = (f32[2,1,256]{2,1,0:T(1,128)}, f32[2,1,256]{2,1,0:T(1,128)S(1)}, u32[]{:S(2)}, u32[]{:S(2)}) collective-permute-start(f32[2,1,256]{2,1,0:T(1,128)} %get-tuple-element.9), channel_id=1, source_target_pairs={{0,1},{1,0},{2,3},{3,2},{4,5},{5,4},{6,7},{7,6},{8,9},{9,8},{10,11... | collective-permute-start | bytes 6152 | tf_op jit(solution)/shard_map/ppermute | solution.py:296
  24.8 15.2 %collective-permute-start.4 = (f32[256,512]{1,0:T(8,128)S(1)}, f32[256,512]{1,0:T(8,128)S(1)}, u32[]{:S(2)}, u32[]{:S(2)}) collective-permute-start(f32[256,512]{1,0:T(8,128)S(1)} %dynamic-slice_bitcast_fusion), channel_id=1, source_target_pairs={{0,2},{1,3},{2,0},{3,1},{4,6},{5,7},{6,4},{7,5},{8,10},{9,11},{10,... | collective-permute-start | bytes 1572872 | tf_op jit(solution)/shard_map/ppermute | solution.py:306
  27.8 12.2 %collective-permute-start.7 = (f32[1,256]{1,0:T(1,128)S(1)}, f32[1,256]{1,0:T(1,128)S(1)}, u32[]{:S(2)}, u32[]{:S(2)}) collective-permute-start(f32[1,256]{1,0:T(1,128)S(1)} %dynamic-slice_bitcast_fusion.2), channel_id=1, source_target_pairs={{0,2},{1,3},{2,0},{3,1},{4,6},{5,7},{6,4},{7,5},{8,10},{9,11},{10,... | collective-permute-start | bytes 3080 | tf_op jit(solution)/shard_map/ppermute | solution.py:307
  40.0 17.0 %copy-start = (f32[2,1,256]{2,1,0:T(1,128)S(1)}, f32[2,1,256]{2,1,0:T(1,128)}, u32[]{:S(2)}) copy-start(f32[2,1,256]{2,1,0:T(1,128)} %get-tuple-element.8) | copy-start | bytes 6148
  41.0 14.2 %collective-permute-start.3 = (f32[256,512]{1,0:T(8,128)S(1)}, f32[256,512]{1,0:T(8,128)S(1)}, u32[]{:S(2)}, u32[]{:S(2)}) collective-permute-start(f32[256,512]{1,0:T(8,128)S(1)} %get-tuple-element.15), channel_id=1, source_target_pairs={{0,2},{1,3},{4,6},{5,7},{8,10},{9,11},{12,14},{13,15},{16,18},{17,... | collective-permute-start | bytes 1572872 | tf_op jit(solution)/shard_map/ppermute | solution.py:318
  44.7 20.1 %collective-permute-start.6 = (f32[2,256,512]{2,1,0:T(8,128)}, f32[2,256,512]{2,1,0:T(8,128)}, u32[]{:S(2)}, u32[]{:S(2)}) collective-permute-start(f32[2,256,512]{2,1,0:T(8,128)} %get-tuple-element.10), channel_id=1, source_target_pairs={{0,1},{2,3},{4,5},{6,7},{8,9},{10,11},{12,13},{14,15},{16,17},{18,... | collective-permute-start | bytes 3145736 | tf_op jit(solution)/shard_map/ppermute | solution.py:321
  55.3 9.5 %collective-permute-start.5 = (f32[2,256,512]{2,1,0:T(8,128)S(1)}, f32[2,256,512]{2,1,0:T(8,128)}, u32[]{:S(2)}, u32[]{:S(2)}) collective-permute-start(f32[2,256,512]{2,1,0:T(8,128)S(1)} %pad_maximum_fusion.1), channel_id=1, source_target_pairs={{2,3},{3,2},{6,7},{7,6},{10,11},{11,10},{14,15},{15,14},{18,19},{1... | collective-permute-start | bytes 3145736 | tf_op jit(solution)/shard_map/ppermute | solution.py:320
  57.0 7.8 %collective-permute-start = (f32[2,1,256]{2,1,0:T(1,128)S(1)}, f32[2,1,256]{2,1,0:T(1,128)S(1)}, u32[]{:S(2)}, u32[]{:S(2)}) collective-permute-start(f32[2,1,256]{2,1,0:T(1,128)S(1)} %copy-done), channel_id=1, source_target_pairs={{0,1},{2,3},{4,5},{6,7},{8,9},{10,11},{12,13},{14,15},{16,17},{18,... | collective-permute-start | bytes 6152 | tf_op jit(solution)/shard_map/ppermute | solution.py:326
Sparse Core Ops, SparseCore 0:
  41.2 75.0 all-gather.2

commit v2 on v1

--- a/solution.py
+++ b/solution.py
@@ -143,8 +143,10 @@
     r_ref[0] = reach
 
 
-def suffix_final_kernel(group, length, a_ref, r_ref, s_ref, z_ref, gain_ref, out_ref):
-    attended = a_ref[0] + dot3(split(r_ref[0]), split(s_ref[0]), NN)
+def suffix_final_kernel(group, slot, length, a_ref, r_ref, s_ref, t_ref, z_ref, gain_ref, out_ref):
+    attended = a_ref[0] + dot3(
+        split(r_ref[0]), split(jnp.concatenate([s_ref[0], t_ref[0]], axis=1)), NN
+    )
     alive = alive_column(0, length[pl.program_id(0)], CHUNK)
     out_ref[0] = gated(attended, z_ref[0], gain_ref[...], alive)
 
@@ -232,20 +234,21 @@
     )(head, q, k, g, v)
 
 
-def suffix_final(group, length, attended, reach, finals, z, gain):
+def suffix_final(group, slot, length, attended, reach, finals, others, z, gain):
     count = attended.shape[0]
-    wide = pl.BlockSpec((1, CHUNK, DVH), lambda i, group, length: (i, 0, 0))
+    wide = pl.BlockSpec((1, CHUNK, DVH), lambda i, group, slot, length: (i, 0, 0))
     return pl.pallas_call(
         suffix_final_kernel,
         grid_spec=pltpu.PrefetchScalarGridSpec(
-            num_scalar_prefetch=2,
+            num_scalar_prefetch=3,
             grid=(count,),
             in_specs=[
                 wide,
-                pl.BlockSpec((1, CHUNK, KEY_CHANNELS), lambda i, group, length: (i, 0, 0)),
-                pl.BlockSpec((1, KEY_CHANNELS, DVH), lambda i, group, length: (group[i], 0, 0)),
+                pl.BlockSpec((1, CHUNK, KEY_CHANNELS), lambda i, group, slot, length: (i, 0, 0)),
+                pl.BlockSpec((1, KEY_CHANNELS, DVH // 2), lambda i, group, slot, length: (group[i], 0, 0)),
+                pl.BlockSpec((1, KEY_CHANNELS, DVH // 2), lambda i, group, slot, length: (slot[i], 0, 0)),
                 wide,
-                pl.BlockSpec((1, DVH), lambda i, group, length: (0, 0)),
+                pl.BlockSpec((1, DVH), lambda i, group, slot, length: (0, 0)),
             ],
             out_specs=wide,
         ),
@@ -253,7 +256,23 @@
         compiler_params=pltpu.CompilerParams(**PARAMS),
         cost_estimate=cost(4e9, 8e6),
         name="suffix_final",
-    )(group, length, attended, reach, finals, z, gain)
+    )(group, slot, length, attended, reach, finals, others, z, gain)
+
+
+def gather_by_permutes(part, group):
+    def shift(value, step, sources):
+        return lax.ppermute(value, "req", [(2 * z + y, 2 * (z + step) + y) for z in sources for y in (0, 1)])
+
+    up, down = [part], [part]
+    for k in (1, 2, 3):
+        up.append(shift(up[-1], 1, range(k - 1, 3)))
+        down.append(shift(down[-1], -1, range(1, 5 - k)))
+    along = [part] + [up[k] + down[4 - k] for k in (1, 2, 3)]
+    swap = [(i, i ^ 1) for i in range(8)]
+    slots = [x for value in along for x in (value, lax.ppermute(value, "req", swap))]
+    me = lax.axis_index("req")
+    behind = lax.rem(me // 2 - group // 2 + 4, 4)
+    return jnp.stack(slots), 2 * behind + jnp.abs(lax.rem(me, 2) - lax.rem(group, 2))
 
 
 def fade_state(offset, state):
@@ -309,7 +328,13 @@
     late_state = jnp.where(chip == 0, far_state, kept_state)
     late_offset = jnp.where(chip == 0, far_offset, kept_offset)
     final = fade_state(late_offset, early_state) + late_state
-    finals = lax.all_gather(final[None], "req", axis=0, tiled=True)
+    half = DVH // 2
+    finals = lax.all_gather(final[None, :, :half], "req", axis=0, tiled=True)
+    if lax.axis_size("req") == 8:
+        others, slot = gather_by_permutes(final[:, half:], request_group)
+    else:
+        others = lax.all_gather(final[None, :, half:], "req", axis=0, tiled=True)
+        slot = request_group
 
     suffix_attended, suffix_reach = suffix_local(
         rank.astype(jnp.int32)[None], suffix_query, suffix_key, suffix_gate_logit, suffix_value
@@ -342,7 +367,7 @@
         gain,
     )
     suffix_result = suffix_final(
-        request_group, suffix_len, suffix_attended, suffix_reach, finals, suffix_out_gate, gain
+        request_group, slot, suffix_len, suffix_attended, suffix_reach, finals, others, suffix_out_gate, gain
     )
     return (prompt_result, suffix_result)
 

time: 130 us -> 156 us (1.20)
  starting transfers between devices: 12.6 us -> 27 us
  waiting for transfers between devices: 37.5 us -> 45.2 us
  local copies, waits for them, and re-layouts: 1.59 us -> 4.54 us
    ppermute x0 -> x10, waiting for transfers between devices: none -> 19.6 us  [the longest x6 16.6 us: shift(): lax.ppermute(value, 'req', [(2 * z + y, 2 * (z + step) + y) for z in sour...]
    ppermute x0 -> x10, starting transfers between devices: none -> 14.6 us  [the longest x6 9.87 us: shift(): lax.ppermute(value, 'req', [(2 * z + y, 2 * (z + step) + y) for z in sour...]
    ppermute x1, waiting for transfers between devices: 8.2 us -> 0.01 us  [local(): rest = lax.ppermute(kept_state, 'seq', [(0, 2), (1, 3)])]
    all_gather x1, waiting for transfers between devices: 17.1 us -> 13.5 us  [local(): finals = lax.all_gather(final[None, :, :half], 'req', axis=0, tiled=True)]
  transfers between devices with their start and end apart: 9 -> 19, of which waited for: 3 -> 7; matrix products, arithmetic and copies ran while one was open for 3% -> 5% of each run, Pallas kernels for 34% -> 28%
where the time goes in v2:
time: 156 us
  Pallas kernels  56.3 us (36%)
  waiting for transfers between devices  45.2 us (29%)
  starting transfers between devices  27 us (17%)
  between operations  14.9 us (10%)
  other arithmetic  7.65 us (5%)
  local copies, waits for them, and re-layouts  4.54 us (3%)
    pallas_call x1, Pallas kernels, prompt_attention(): pl.pallas_call(prompt_kernel, grid_spec=pltpu.PrefetchScalarGridSpec(num_...  30.8 us
    ppermute x6, waiting for transfers between devices, shift(): lax.ppermute(value, 'req', [(2 * z + y, 2 * (z + step) + y) for z in sour...  16.6 us
    all_gather x1, waiting for transfers between devices, local(): finals = lax.all_gather(final[None, :, :half], 'req', axis=0, tiled=True)  13.5 us
    pallas_call x2, Pallas kernels, local_states(): pl.pallas_call(state_kernel, grid_spec=pltpu.PrefetchScalarGridSpec(num_s...  13 us
    ppermute x1, waiting for transfers between devices, local(): far_offset = lax.ppermute(pick(chip_offset, 1 - chip), 'seq', across_chip)  12.1 us
    ppermute x6, starting transfers between devices, shift(): lax.ppermute(value, 'req', [(2 * z + y, 2 * (z + step) + y) for z in sour...  9.87 us
    pallas_call x1, Pallas kernels, suffix_local(): pl.pallas_call(suffix_local_kernel, grid_spec=pltpu.PrefetchScalarGridSpe...  6.44 us
    pallas_call x1, Pallas kernels, suffix_final(): pl.pallas_call(suffix_final_kernel, grid_spec=pltpu.PrefetchScalarGridSpe...  6.03 us
  transfers between devices with their start and end apart: 19, of which 7 were waited for; matrix products, arithmetic and copies ran while one was open for 5% of the time, Pallas kernels for 28%

profile of v2, /device:TPU:0, one launch (start us, length us, event | category | flops | bytes accessed | tf_op | source)
XLA Modules:
  0.0 155.6 jit_solution(4993560316104024468)
XLA Ops:
  7.2 0.0 all-gather.3.cloned.1.call-start
  7.2 0.6 add_subtract_fusion
  8.5 0.6 pad_add_fusion.info
  9.0 6.5 %local_states.3 = (f32[2,256,512]{2,1,0:T(8,128)}, f32[2,1,256]{2,1,0:T(1,128)}) custom-call(s32[2]{0:T(128)} %get-tuple-element.29.heads, s32[2]{0:T(128)} %pad_add_fusion.info, bf16[1,1024,1024]{2,1,0:T(8,128)(2,1)} %k_ref.6, bf16[1,1024,1024]{2,1,0:T(8,128)(2,1)} %g_ref.6, bf16[1,1024,2048]{2,1,0:T(8,128)(2,1)} %v_ref.6), custom_call_target="tpu_custom_call" | custom-call | flops 4000000000 | bytes 5000000 | tf_op jit(solution)/shard_map/local_states/pallas_call | solution.py:166
  15.5 0.5 collective-permute-start.2
  16.0 0.1 collective-permute-start.1
  16.0 6.5 %local_states.2 = (f32[2,256,512]{2,1,0:T(8,128)}, f32[2,1,256]{2,1,0:T(1,128)}) custom-call(s32[2]{0:T(128)} %get-tuple-element.30.heads, s32[2]{0:T(128)} %pad_add_fusion.info, bf16[1,1024,1024]{2,1,0:T(8,128)(2,1)} %k_ref.6, bf16[1,1024,1024]{2,1,0:T(8,128)(2,1)} %g_ref.6, bf16[1,1024,2048]{2,1,0:T(8,128)(2,1)} %v_ref.6), custom_call_target="tpu_custom_call" | custom-call | flops 4000000000 | bytes 5000000 | tf_op jit(solution)/shard_map/local_states/pallas_call | solution.py:166
  22.5 0.7 fusion.7
  23.2 0.0 collective-permute-done.2
  23.2 1.4 select_add_fusion
  24.7 3.0 %collective-permute-start.4 = (f32[256,512]{1,0:T(8,128)S(1)}, f32[256,512]{1,0:T(8,128)S(1)}, u32[]{:S(2)}, u32[]{:S(2)}) collective-permute-start(f32[256,512]{1,0:T(8,128)S(1)} %dynamic-slice_bitcast_fusion), channel_id=1, source_target_pairs={{0,2},{1,3},{2,0},{3,1},{4,6},{5,7},{6,4},{7,5},{8,10},{9,11},{10,... | collective-permute-start | bytes 1572872 | tf_op jit(solution)/shard_map/ppermute | solution.py:325
  27.7 0.1 collective-permute-start.7
  27.8 12.1 %collective-permute-done.7 = f32[1,256]{1,0:T(1,128)S(1)} collective-permute-done((f32[1,256]{1,0:T(1,128)S(1)}, f32[1,256]{1,0:T(1,128)S(1)}, u32[]{:S(2)}, u32[]{:S(2)}) %collective-permute-start.7) | collective-permute-done | bytes 1056 | tf_op jit(solution)/shard_map/ppermute | solution.py:326
  40.0 0.0 collective-permute-done.4
  40.0 0.1 select_add_fusion.1
  40.1 0.7 fusion.6
  40.9 1.4 collective-permute-start.10
  42.3 8.3 %collective-permute-done.10 = f32[256,256]{1,0:T(8,128)S(1)} collective-permute-done((f32[256,256]{1,0:T(8,128)S(1)}, f32[256,256]{1,0:T(8,128)S(1)}, u32[]{:S(2)}, u32[]{:S(2)}) %collective-permute-start.10) | collective-permute-done | bytes 262176 | tf_op jit(solution)/shard_map/ppermute | solution.py:264
  50.6 1.3 collective-permute-start.11
  51.9 1.5 collective-permute-start.8
  53.4 4.5 %collective-permute-start.9 = (f32[256,256]{1,0:T(8,128)S(1)}, f32[256,256]{1,0:T(8,128)S(1)}, u32[]{:S(2)}, u32[]{:S(2)}) collective-permute-start(f32[256,256]{1,0:T(8,128)S(1)} %get-tuple-element.24), channel_id=1, source_target_pairs={{0,8},{4,12},{8,16},{12,20},{16,24},{20,28},{1,9},{5,13},{9,17},{1... | collective-permute-start | bytes 786440 | tf_op jit(solution)/shard_map/ppermute | solution.py:264
  57.9 1.3 collective-permute-done.11
  59.3 1.3 collective-permute-start.12
  60.6 1.2 collective-permute-done.9
  61.8 5.7 %collective-permute-done.12 = f32[256,256]{1,0:T(8,128)S(1)} collective-permute-done((f32[256,256]{1,0:T(8,128)S(1)}, f32[256,256]{1,0:T(8,128)S(1)}, u32[]{:S(2)}, u32[]{:S(2)}) %collective-permute-start.12) | collective-permute-done | bytes 262176 | tf_op jit(solution)/shard_map/ppermute | solution.py:264
  67.6 1.2 collective-permute-start.13
  68.8 0.7 collective-permute-start.14
  69.4 3.4 %collective-permute-start.3 = (f32[256,512]{1,0:T(8,128)S(1)}, f32[256,512]{1,0:T(8,128)S(1)}, u32[]{:S(2)}, u32[]{:S(2)}) collective-permute-start(f32[256,512]{1,0:T(8,128)S(1)} %get-tuple-element.21), channel_id=1, source_target_pairs={{0,2},{1,3},{4,6},{5,7},{8,10},{9,11},{12,14},{13,15},{16,18},{17,... | collective-permute-start | bytes 1572872 | tf_op jit(solution)/shard_map/ppermute | solution.py:343
  72.9 3.0 %collective-permute-done.13 = f32[256,256]{1,0:T(8,128)S(1)} collective-permute-done((f32[256,256]{1,0:T(8,128)S(1)}, f32[256,256]{1,0:T(8,128)S(1)}, u32[]{:S(2)}, u32[]{:S(2)}) %collective-permute-start.13) | collective-permute-done | bytes 262176 | tf_op jit(solution)/shard_map/ppermute | solution.py:272
  76.0 1.5 collective-permute-start.15
  77.5 2.2 %collective-permute-start.6 = (f32[2,256,512]{2,1,0:T(8,128)S(1)}, f32[2,256,512]{2,1,0:T(8,128)}, u32[]{:S(2)}, u32[]{:S(2)}) collective-permute-start(f32[2,256,512]{2,1,0:T(8,128)S(1)} %copy-done), channel_id=1, source_target_pairs={{0,1},{2,3},{4,5},{6,7},{8,9},{10,11},{12,13},{14,15},{16,17},{18,... | collective-permute-start | bytes 3145736 | tf_op jit(solution)/shard_map/ppermute | solution.py:346
  79.8 1.3 collective-permute-start
  81.1 0.7 collective-permute-start.16
  81.8 1.0 pad_maximum_fusion.1
  82.8 1.7 %collective-permute-start.5 = (f32[2,256,512]{2,1,0:T(8,128)}, f32[2,256,512]{2,1,0:T(8,128)}, u32[]{:S(2)}, u32[]{:S(2)}) collective-permute-start(f32[2,256,512]{2,1,0:T(8,128)} %pad_maximum_fusion.1), channel_id=1, source_target_pairs={{2,3},{3,2},{6,7},{7,6},{10,11},{11,10},{14,15},{15,14},{18,19},{1... | collective-permute-start | bytes 3145736 | tf_op jit(solution)/shard_map/ppermute | solution.py:345
  84.6 0.7 bitcast_dynamic-update-slice_fusion.1
  85.3 1.4 copy-done.1
  86.7 0.5 collective-permute-start.17
  87.2 6.4 %suffix_local.1 = (f32[4,256,512]{2,1,0:T(8,128)}, f32[4,256,256]{2,1,0:T(8,128)}) custom-call(s32[1]{0:T(128)} %bitcast.9.head, bf16[4,256,1024]{2,1,0:T(8,128)(2,1)} %q_ref.3, bf16[4,256,1024]{2,1,0:T(8,128)(2,1)} %k_ref.7, bf16[4,256,1024]{2,1,0:T(8,128)(2,1)} %g_ref.7, bf16[4,256,512]{2,1,0:T(8,128)(2,1)} %v_ref.7), custom_call_target="tpu_custom_call" | custom-call | flops 6000000000 | bytes 4000000 | tf_op jit(solution)/shard_map/suffix_local/pallas_call | solution.py:219
  93.7 0.0 all-gather.3.cloned.1.call-update
  93.7 0.5 fusion.4.slot
  94.3 0.7 bitcast_dynamic-update-slice_fusion.t_ref
  95.0 1.6 %select_bitcast_fusion.1 = (f32[2,1,256,512]{3,2,0,1:T(8,128)S(1)}, f32[2,1,256,512]{3,2,0,1:T(8,128)S(1)}) fusion(pred[]{:T(512)S(6)} %eq.16, f32[2,256,512]{2,1,0:T(8,128)} %collective-permute-done.6, f32[2,256,512]{2,1,0:T(8,128)} %collective-permute-done.5, pred[]{:T(512)S(6)} %eq.17, f32[2,256]{1,0:T(2,128)S(1)} %bitcast.52, ...), kind=kLoop, calls=%fused_computation.3 | loop fusion | flops 2883584 | bytes 6295554 | tf_op jit(solution)/shard_map/stack | solution.py:358
  96.7 0.2 pad_maximum_fusion
  96.8 1.6 %copy.16 = f32[2,2,256,512]{3,2,1,0:T(8,128)} copy(f32[2,2,256,512]{3,2,0,1:T(8,128)S(1)} %pad_maximum_fusion) | data formatting | bytes 4194304 | tf_op jit(solution)/shard_map/stack | solution.py:358
  98.4 30.8 %prompt_attention.1 = bf16[1,1024,2048]{2,1,0:T(8,128)(2,1)} custom-call(s32[2]{0:T(128)} %pad_add_fusion.info, bf16[1,1024,1024]{2,1,0:T(8,128)(2,1)} %q_ref.2, bf16[1,1024,1024]{2,1,0:T(8,128)(2,1)} %k_ref.6, bf16[1,1024,1024]{2,1,0:T(8,128)(2,1)} %g_ref.6, bf16[1,1024,2048]{2,1,0:T(8,128)(2,1)} %v_ref.6, bf16[1,1024,2048]{2,1,0:T(8,128)(2,1)} %z_ref.2, ...), custom_call_target="tpu_custom_call" | custom-call | flops 30000001024 | bytes 20000000 | tf_op jit(solution)/shard_map/prompt_attention/pallas_call | solution.py:191
  129.2 13.5 %all-gather.3.cloned.1.call-done = f32[2048,256]{1,0:T(8,128)} async-done(((f32[256,256]{1,0:T(8,128)}), f32[2048,256]{1,0:T(8,128)}) %all-gather.3.cloned.1.call-update) | async-done | bytes 2097168 | tf_op jit(solution)/shard_map/all_gather | solution.py:332
  142.7 6.0 %suffix_final.1 = bf16[4,256,512]{2,1,0:T(8,128)(2,1)} custom-call(s32[4]{0:T(128)} %group.1, s32[4]{0:T(128)} %fusion.4.slot, s32[4]{0:T(128)} %length.1, f32[4,256,512]{2,1,0:T(8,128)} %get-tuple-element.12.a_ref, f32[4,256,256]{2,1,0:T(8,128)} %get-tuple-element.13.r_ref, f32[8,256,256]{2,1,0:T(8,128)} %bitcast.55, ...), custom_call_target="tpu_custom_call" | custom-call | flops 4000000000 | bytes 8000000 | tf_op jit(solution)/shard_map/suffix_final/pallas_call | solution.py:240
  (30 shorter events, 0.3 us)
Async XLA Ops:
  7.2 135.5 %all-gather.3.cloned.1.call-start = ((), (), s32[]{:S(2)}) async-start(), calls=%async_computation | async-start | bytes 2359296 | tf_op jit(solution)/shard_map/all_gather | solution.py:332
  15.5 7.7 %collective-permute-start.2 = (f32[2,256,512]{2,1,0:T(8,128)}, f32[2,256,512]{2,1,0:T(8,128)S(1)}, u32[]{:S(2)}, u32[]{:S(2)}) collective-permute-start(f32[2,256,512]{2,1,0:T(8,128)} %get-tuple-element.11), channel_id=1, source_target_pairs={{0,1},{1,0},{2,3},{3,2},{4,5},{5,4},{6,7},{7,6},{8,9},{9,8},{10,11... | collective-permute-start | bytes 3145736 | tf_op jit(solution)/shard_map/ppermute | solution.py:314
  16.0 6.6 %collective-permute-start.1 = (f32[2,1,256]{2,1,0:T(1,128)}, f32[2,1,256]{2,1,0:T(1,128)S(1)}, u32[]{:S(2)}, u32[]{:S(2)}) collective-permute-start(f32[2,1,256]{2,1,0:T(1,128)} %get-tuple-element.9), channel_id=1, source_target_pairs={{0,1},{1,0},{2,3},{3,2},{4,5},{5,4},{6,7},{7,6},{8,9},{9,8},{10,11... | collective-permute-start | bytes 6152 | tf_op jit(solution)/shard_map/ppermute | solution.py:315
  24.7 15.2 %collective-permute-start.4 = (f32[256,512]{1,0:T(8,128)S(1)}, f32[256,512]{1,0:T(8,128)S(1)}, u32[]{:S(2)}, u32[]{:S(2)}) collective-permute-start(f32[256,512]{1,0:T(8,128)S(1)} %dynamic-slice_bitcast_fusion), channel_id=1, source_target_pairs={{0,2},{1,3},{2,0},{3,1},{4,6},{5,7},{6,4},{7,5},{8,10},{9,11},{10,... | collective-permute-start | bytes 1572872 | tf_op jit(solution)/shard_map/ppermute | solution.py:325
  27.7 12.2 %collective-permute-start.7 = (f32[1,256]{1,0:T(1,128)S(1)}, f32[1,256]{1,0:T(1,128)S(1)}, u32[]{:S(2)}, u32[]{:S(2)}) collective-permute-start(f32[1,256]{1,0:T(1,128)S(1)} %dynamic-slice_bitcast_fusion.2), channel_id=1, source_target_pairs={{0,2},{1,3},{2,0},{3,1},{4,6},{5,7},{6,4},{7,5},{8,10},{9,11},{10,... | collective-permute-start | bytes 3080 | tf_op jit(solution)/shard_map/ppermute | solution.py:326
  40.9 36.7 %copy-start = (f32[2,256,512]{2,1,0:T(8,128)S(1)}, f32[2,256,512]{2,1,0:T(8,128)}, u32[]{:S(2)}) copy-start(f32[2,256,512]{2,1,0:T(8,128)} %get-tuple-element.10) | copy-start | bytes 3145732
  40.9 38.9 %copy-start.2 = (f32[2,1,256]{2,1,0:T(1,128)S(1)}, f32[2,1,256]{2,1,0:T(1,128)}, u32[]{:S(2)}) copy-start(f32[2,1,256]{2,1,0:T(1,128)} %get-tuple-element.8) | copy-start | bytes 6148
  40.9 9.7 %collective-permute-start.10 = (f32[256,256]{1,0:T(8,128)S(1)}, f32[256,256]{1,0:T(8,128)S(1)}, u32[]{:S(2)}, u32[]{:S(2)}) collective-permute-start(f32[256,256]{1,0:T(8,128)S(1)} %get-tuple-element.24), channel_id=1, source_target_pairs={{8,0},{12,4},{16,8},{20,12},{24,16},{28,20},{9,1},{13,5},{17,9},{2... | collective-permute-start | bytes 786440 | tf_op jit(solution)/shard_map/ppermute | solution.py:264
  50.6 8.7 %collective-permute-start.11 = (f32[256,256]{1,0:T(8,128)S(1)}, f32[256,256]{1,0:T(8,128)S(1)}, u32[]{:S(2)}, u32[]{:S(2)}) collective-permute-start(f32[256,256]{1,0:T(8,128)S(1)} %collective-permute-done.10), channel_id=1, source_target_pairs={{8,0},{12,4},{16,8},{20,12},{9,1},{13,5},{17,9},{21,13},{10,2},{14... | collective-permute-start | bytes 786440 | tf_op jit(solution)/shard_map/ppermute | solution.py:264
  51.9 8.7 %collective-permute-start.8 = (f32[256,256]{1,0:T(8,128)S(1)}, f32[256,256]{1,0:T(8,128)S(1)}, u32[]{:S(2)}, u32[]{:S(2)}) collective-permute-start(f32[256,256]{1,0:T(8,128)S(1)} %get-tuple-element.24), channel_id=1, source_target_pairs={{0,4},{4,0},{8,12},{12,8},{16,20},{20,16},{24,28},{28,24},{1,5},{5... | collective-permute-start | bytes 786440 | tf_op jit(solution)/shard_map/ppermute | solution.py:272
  53.4 8.4 %collective-permute-start.9 = (f32[256,256]{1,0:T(8,128)S(1)}, f32[256,256]{1,0:T(8,128)S(1)}, u32[]{:S(2)}, u32[]{:S(2)}) collective-permute-start(f32[256,256]{1,0:T(8,128)S(1)} %get-tuple-element.24), channel_id=1, source_target_pairs={{0,8},{4,12},{8,16},{12,20},{16,24},{20,28},{1,9},{5,13},{9,17},{1... | collective-permute-start | bytes 786440 | tf_op jit(solution)/shard_map/ppermute | solution.py:264
  59.3 8.3 %collective-permute-start.12 = (f32[256,256]{1,0:T(8,128)S(1)}, f32[256,256]{1,0:T(8,128)S(1)}, u32[]{:S(2)}, u32[]{:S(2)}) collective-permute-start(f32[256,256]{1,0:T(8,128)S(1)} %collective-permute-done.11), channel_id=1, source_target_pairs={{8,0},{12,4},{9,1},{13,5},{10,2},{14,6},{11,3},{15,7}} | collective-permute-start | bytes 786440 | tf_op jit(solution)/shard_map/ppermute | solution.py:264
  67.6 8.3 %collective-permute-start.13 = (f32[256,256]{1,0:T(8,128)S(1)}, f32[256,256]{1,0:T(8,128)S(1)}, u32[]{:S(2)}, u32[]{:S(2)}) collective-permute-start(f32[256,256]{1,0:T(8,128)S(1)} %get-tuple-element.19), channel_id=1, source_target_pairs={{0,4},{4,0},{8,12},{12,8},{16,20},{20,16},{24,28},{28,24},{1,5},{5... | collective-permute-start | bytes 786440 | tf_op jit(solution)/shard_map/ppermute | solution.py:272
  68.8 7.2 %collective-permute-start.14 = (f32[256,256]{1,0:T(8,128)S(1)}, f32[256,256]{1,0:T(8,128)S(1)}, u32[]{:S(2)}, u32[]{:S(2)}) collective-permute-start(f32[256,256]{1,0:T(8,128)S(1)} %collective-permute-done.9), channel_id=1, source_target_pairs={{8,16},{12,20},{16,24},{20,28},{9,17},{13,21},{17,25},{21,29},{10,... | collective-permute-start | bytes 786440 | tf_op jit(solution)/shard_map/ppermute | solution.py:264
  69.4 12.3 %collective-permute-start.3 = (f32[256,512]{1,0:T(8,128)S(1)}, f32[256,512]{1,0:T(8,128)S(1)}, u32[]{:S(2)}, u32[]{:S(2)}) collective-permute-start(f32[256,512]{1,0:T(8,128)S(1)} %get-tuple-element.21), channel_id=1, source_target_pairs={{0,2},{1,3},{4,6},{5,7},{8,10},{9,11},{12,14},{13,15},{16,18},{17,... | collective-permute-start | bytes 1572872 | tf_op jit(solution)/shard_map/ppermute | solution.py:343
  76.0 8.6 %collective-permute-start.15 = (f32[256,256]{1,0:T(8,128)S(1)}, f32[256,256]{1,0:T(8,128)S(1)}, u32[]{:S(2)}, u32[]{:S(2)}) collective-permute-start(f32[256,256]{1,0:T(8,128)S(1)} %get-tuple-element.17), channel_id=1, source_target_pairs={{0,4},{4,0},{8,12},{12,8},{16,20},{20,16},{24,28},{28,24},{1,5},{5... | collective-permute-start | bytes 786440 | tf_op jit(solution)/shard_map/ppermute | solution.py:272
  77.5 17.5 %collective-permute-start.6 = (f32[2,256,512]{2,1,0:T(8,128)S(1)}, f32[2,256,512]{2,1,0:T(8,128)}, u32[]{:S(2)}, u32[]{:S(2)}) collective-permute-start(f32[2,256,512]{2,1,0:T(8,128)S(1)} %copy-done), channel_id=1, source_target_pairs={{0,1},{2,3},{4,5},{6,7},{8,9},{10,11},{12,13},{14,15},{16,17},{18,... | collective-permute-start | bytes 3145736 | tf_op jit(solution)/shard_map/ppermute | solution.py:346
  79.8 14.5 %collective-permute-start = (f32[2,1,256]{2,1,0:T(1,128)S(1)}, f32[2,1,256]{2,1,0:T(1,128)S(1)}, u32[]{:S(2)}, u32[]{:S(2)}) collective-permute-start(f32[2,1,256]{2,1,0:T(1,128)S(1)} %copy-done.2), channel_id=1, source_target_pairs={{0,1},{2,3},{4,5},{6,7},{8,9},{10,11},{12,13},{14,15},{16,17},{18,... | collective-permute-start | bytes 6152 | tf_op jit(solution)/shard_map/ppermute | solution.py:351
  81.1 3.5 %collective-permute-start.16 = (f32[256,256]{1,0:T(8,128)S(1)}, f32[256,256]{1,0:T(8,128)S(1)}, u32[]{:S(2)}, u32[]{:S(2)}) collective-permute-start(f32[256,256]{1,0:T(8,128)S(1)} %collective-permute-done.14), channel_id=1, source_target_pairs={{16,24},{20,28},{17,25},{21,29},{18,26},{22,30},{19,27},{23,31}} | collective-permute-start | bytes 786440 | tf_op jit(solution)/shard_map/ppermute | solution.py:264
  82.8 12.2 %collective-permute-start.5 = (f32[2,256,512]{2,1,0:T(8,128)}, f32[2,256,512]{2,1,0:T(8,128)}, u32[]{:S(2)}, u32[]{:S(2)}) collective-permute-start(f32[2,256,512]{2,1,0:T(8,128)} %pad_maximum_fusion.1), channel_id=1, source_target_pairs={{2,3},{3,2},{6,7},{7,6},{10,11},{11,10},{14,15},{15,14},{18,19},{1... | collective-permute-start | bytes 3145736 | tf_op jit(solution)/shard_map/ppermute | solution.py:345
  85.3 1.4 copy-start.1
  86.7 7.6 %collective-permute-start.17 = (f32[256,256]{1,0:T(8,128)}, f32[256,256]{1,0:T(8,128)S(1)}, u32[]{:S(2)}, u32[]{:S(2)}) collective-permute-start(f32[256,256]{1,0:T(8,128)} %get-tuple-element.15), channel_id=1, source_target_pairs={{0,4},{4,0},{8,12},{12,8},{16,20},{20,16},{24,28},{28,24},{1,5},{5... | collective-permute-start | bytes 786440 | tf_op jit(solution)/shard_map/ppermute | solution.py:272
  87.2 6.5 %copy-start.3 = (s32[4]{0:T(128)S(1)}, s32[4]{0:T(128)}, u32[]{:S(2)}) copy-start(s32[4]{0:T(128)} %group.1) | copy-start | bytes 52
Sparse Core Ops, SparseCore 0:
  93.8 48.8 all-gather.2
